TPU v7x, 256 devices: a whole 4x4x8 slice. The times are simulated.
256 devices in a mesh: ctx: 8 (over z), exp: 32 (over y, x, core).
Axes of the slice: x: 4, y: 4, z: 8, core: 2. Of those that a mesh axis runs over, the one named last changes fastest.
Arguments:
- query_rows: bfloat16 [6144, 4096], P('ctx', 'exp'), may hold values from -6 to 6
- key_rows: bfloat16 [6144, 4096], P('ctx', 'exp'), may hold values from -6 to 6
- value_rows: bfloat16 [6144, 4096], P('ctx', 'exp'), may hold values from -6 to 6
- log_decay: float32 [32, 6144], P('exp', 'ctx'), may hold values from -1 to 0
- residual: bfloat16 [6144, 3072], P(('ctx', 'exp')), may hold values from -20 to 20
- norm_gain: float32 [3072], replicated, may hold values from 0.1 to 1.9
- out_grad: bfloat16 [6144, 3072], P(('ctx', 'exp')), may hold values from -6 to 6
- experts_of: int32 [6144, 2], P(('ctx', 'exp')), may hold values from 0 to 31, all different within a row; in each aligned block of 24 rows (0 to 23, 24 to 47, ...) at most 2 rows name the same one
- route_weight: float32 [6144, 2], P(('ctx', 'exp')), may hold values from 0.1 to 0.9
- output_weight: bfloat16 [4096, 3072], P('exp'), may hold values from -0.09375 to 0.09375
- expert_gate: bfloat16 [32, 3072, 4608], P('exp', None, 'ctx'), may hold values from -0.109375 to 0.109375
- expert_up: bfloat16 [32, 3072, 4608], P('exp', None, 'ctx'), may hold values from -0.109375 to 0.109375
- expert_down: bfloat16 [32, 4608, 3072], P('exp', 'ctx'), may hold values from -0.09375 to 0.09375
Outputs:
- query_grad: bfloat16 [6144, 4096], P('ctx', 'exp')
- key_grad: bfloat16 [6144, 4096], P('ctx', 'exp')
- value_grad: bfloat16 [6144, 4096], P('ctx', 'exp')
Inputs may be any that keep to these rules, and one draw needn't show every extreme that they name: `experts_of`: in each aligned block of 24 tokens (the tokens of one device) no expert is named by more than 2 tokens, a bound that some block reaches; a token's two experts differ.
All inputs are finite; a program needn't handle non-finite values.
Results may differ from a plain program's by a relative error of at most 0.017.
Values may be sent and summed in bfloat16 or wider, within the bound.
No kernel may reach another device: no remote copies, remote signals or barrier semaphores. Data moves between devices by JAX's collectives and lax.ppermute only.
A program may use at most 128 MiB of HBM per device.

v0:
```python
import math
import jax
import jax.numpy as jnp
from jax import lax
from jax.sharding import PartitionSpec as P


def prefix(part, axis, combine, identity, reverse):
    count = lax.axis_size(axis)
    place = lax.axis_index(axis)
    ahead = count - 1 - place if reverse else place
    gathered = jax.tree.map(lambda a: lax.all_gather(a, axis), part)
    state = jax.tree.map(lambda a, e: jnp.zeros_like(a) + jnp.asarray(e, a.dtype), part, identity)

    def one(turn, state):
        source = count - 1 - turn if reverse else turn
        return combine(
            state, jax.tree.map(lambda a: lax.dynamic_index_in_dim(a, source, 0, False), gathered)
        )

    return lax.fori_loop(0, ahead, one, state)


def normalize(residual, norm_gain):
    residual_f = residual.astype(jnp.float32)
    factor = lax.rsqrt(jnp.mean(residual_f * residual_f, axis=-1, keepdims=True) + 1e-05)
    return (residual_f, factor, (residual_f * factor * norm_gain).astype(jnp.bfloat16))


def slot_table(experts_of, count, capacity):
    flat_ids = experts_of.reshape(-1)
    matches = (flat_ids[:, None] == jnp.arange(count, dtype=jnp.int32)[None, :]).astype(jnp.int32)
    before = jnp.cumsum(matches, axis=0, dtype=jnp.int32) - matches
    target = flat_ids * capacity + jnp.sum(before * matches, axis=1, dtype=jnp.int32)
    slots = jnp.arange(count * capacity, dtype=jnp.int32)
    return (slots[:, None] == target[None, :]).astype(jnp.bfloat16)


def expert_rows(row_block, gate_mat, up_mat, down_mat):
    features = gate_mat.shape[0]
    row_input = row_block[:, :features]
    row_grad = row_block[:, features:]
    gate_pre = jnp.dot(row_input, gate_mat, preferred_element_type=jnp.float32)
    up_pre = jnp.dot(row_input, up_mat, preferred_element_type=jnp.float32)
    hidden_grad = lax.dot_general(
        row_grad, down_mat, (((1,), (1,)), ((), ())), preferred_element_type=jnp.float32
    )
    gate_sig = jax.nn.sigmoid(gate_pre)
    gate_grad = (hidden_grad * up_pre * gate_sig * (1.0 + gate_pre * (1.0 - gate_sig))).astype(
        jnp.bfloat16
    )
    up_grad = (hidden_grad * gate_pre * gate_sig).astype(jnp.bfloat16)
    first = lax.dot_general(
        gate_grad, gate_mat, (((1,), (1,)), ((), ())), preferred_element_type=jnp.float32
    )
    second = lax.dot_general(
        up_grad, up_mat, (((1,), (1,)), ((), ())), preferred_element_type=jnp.float32
    )
    return first + second


def block_terms(query_part, key_part, value_part, grad_part, log_steps, score_scale):
    levels = jnp.cumsum(log_steps)
    block_total = levels[-1]
    from_start = jnp.exp(levels)
    to_end = jnp.exp(block_total - levels)
    key_state = lax.dot_general(
        key_part.astype(jnp.float32) * to_end[:, None],
        value_part.astype(jnp.float32),
        (((0,), (0,)), ((), ())),
        precision=lax.Precision.HIGHEST,
    )
    adjoint = score_scale * lax.dot_general(
        query_part.astype(jnp.float32) * from_start[:, None],
        grad_part.astype(jnp.float32),
        (((0,), (0,)), ((), ())),
        precision=lax.Precision.HIGHEST,
    )
    return (levels, jnp.exp(block_total), key_state, adjoint)


def block_grads(
    query_part, key_part, value_part, grad_part, levels, state_in, adjoint_out, score_scale
):
    block_total = levels[-1]
    from_start = jnp.exp(levels)
    to_end = jnp.exp(block_total - levels)
    token_position = jnp.arange(levels.shape[0], dtype=jnp.int32)
    causal = token_position[:, None] >= token_position[None, :]
    fading = jnp.exp(jnp.where(causal, levels[:, None] - levels[None, :], -jnp.inf))
    scores = lax.dot_general(
        query_part, key_part, (((1,), (1,)), ((), ())), preferred_element_type=jnp.float32
    )
    attn_probs = (score_scale * scores * fading).astype(jnp.bfloat16)
    grad_scores = lax.dot_general(
        grad_part, value_part, (((1,), (1,)), ((), ())), preferred_element_type=jnp.float32
    )
    pull_weights = (score_scale * grad_scores * fading).astype(jnp.bfloat16)
    grad_f = grad_part.astype(jnp.float32)
    query_out = jnp.dot(pull_weights, key_part, preferred_element_type=jnp.float32)
    query_out = query_out + score_scale * from_start[:, None] * lax.dot_general(
        grad_f, state_in, (((1,), (1,)), ((), ())), precision=lax.Precision.HIGHEST
    )
    key_out = lax.dot_general(
        pull_weights, query_part, (((0,), (0,)), ((), ())), preferred_element_type=jnp.float32
    )
    key_out = key_out + to_end[:, None] * lax.dot_general(
        value_part.astype(jnp.float32),
        adjoint_out,
        (((1,), (1,)), ((), ())),
        precision=lax.Precision.HIGHEST,
    )
    value_out = lax.dot_general(
        attn_probs, grad_part, (((0,), (0,)), ((), ())), preferred_element_type=jnp.float32
    )
    value_out = value_out + to_end[:, None] * jnp.dot(
        key_part.astype(jnp.float32), adjoint_out, precision=lax.Precision.HIGHEST
    )
    return (
        query_out.astype(jnp.bfloat16),
        key_out.astype(jnp.bfloat16),
        value_out.astype(jnp.bfloat16),
    )


def chain_link(earlier, following):
    return (earlier[0] * following[0], following[0] * earlier[1] + following[1])


def body(
    query_rows,
    key_rows,
    value_rows,
    log_decay,
    residual,
    norm_gain,
    out_grad,
    experts_of,
    route_weight,
    output_weight,
    expert_gate,
    expert_up,
    expert_down,
):
    ctx_count = lax.axis_size("ctx")
    exp_count = lax.axis_size("exp")
    token_count = residual.shape[0]
    features = residual.shape[1]
    capacity = max(2, 3 * token_count // exp_count)
    residual_f, factor, expert_input = normalize(residual, norm_gain)
    slot_onehot = slot_table(experts_of, exp_count, capacity)
    routed = (route_weight[:, :, None] * out_grad.astype(jnp.float32)[:, None, :]).astype(
        jnp.bfloat16
    )
    inputs = jnp.broadcast_to(expert_input[:, None, :], routed.shape)
    packed = jnp.concatenate([inputs, routed], axis=-1).reshape(2 * token_count, 2 * features)
    outgoing = jnp.dot(slot_onehot, packed, preferred_element_type=jnp.float32).astype(jnp.bfloat16)
    outgoing = outgoing.reshape(exp_count, capacity, 2 * features)
    gate_mat = expert_gate[0]
    up_mat = expert_up[0]
    down_mat = expert_down[0]
    arrived = lax.all_to_all(outgoing, "exp", split_axis=0, concat_axis=0, tiled=True).reshape(
        exp_count * capacity, 2 * features
    )
    partials = expert_rows(
        lax.all_gather(arrived, "ctx", axis=0, tiled=True), gate_mat, up_mat, down_mat
    )
    partials = partials.reshape(ctx_count, exp_count, capacity, features)
    summed = lax.psum_scatter(
        partials.astype(jnp.bfloat16), "ctx", scatter_dimension=0, tiled=True
    ).astype(jnp.float32)
    returned = lax.all_to_all(
        summed[0].astype(jnp.bfloat16), "exp", split_axis=0, concat_axis=0, tiled=True
    )
    per_row = lax.dot_general(
        slot_onehot,
        returned.reshape(exp_count * capacity, features),
        (((0,), (0,)), ((), ())),
        preferred_element_type=jnp.float32,
    )
    moe_grad = jnp.sum(per_row.reshape(token_count, 2, features), axis=1)
    scaled = norm_gain * moe_grad
    unit_rows = residual_f * factor
    total_grad = out_grad.astype(jnp.float32) + factor * (
        scaled - unit_rows * jnp.mean(unit_rows * scaled, axis=-1, keepdims=True)
    )
    resid_grad = total_grad.astype(jnp.bfloat16)
    attn_grad = lax.dot_general(
        lax.all_gather(resid_grad, "exp", axis=0, tiled=True),
        output_weight,
        (((1,), (1,)), ((), ())),
        preferred_element_type=jnp.float32,
    ).astype(jnp.bfloat16)
    block_len = query_rows.shape[0]
    head_size = query_rows.shape[1]
    score_scale = 1.0 / math.sqrt(head_size * block_len * ctx_count)
    levels, block_gain, key_state, adjoint = block_terms(
        query_rows, key_rows, value_rows, attn_grad, log_decay[0], score_scale
    )
    zero_state = jnp.zeros((head_size, head_size), jnp.float32)
    identity = (jnp.ones((), jnp.float32), zero_state)
    state_pair = prefix((block_gain, key_state), "ctx", chain_link, identity, False)
    adjoint_pair = prefix((block_gain, adjoint), "ctx", chain_link, identity, True)
    state_in = state_pair[1]
    adjoint_out = adjoint_pair[1]
    return block_grads(
        query_rows, key_rows, value_rows, attn_grad, levels, state_in, adjoint_out, score_scale
    )


def solution(mesh):
    placed = (
        P("ctx", "exp"),
        P("ctx", "exp"),
        P("ctx", "exp"),
        P("exp", "ctx"),
        P(("ctx", "exp"), None),
        P(),
        P(("ctx", "exp"), None),
        P(("ctx", "exp"), None),
        P(("ctx", "exp"), None),
        P("exp", None),
        P("exp", None, "ctx"),
        P("exp", None, "ctx"),
        P("exp", "ctx", None),
    )
    return jax.shard_map(
        body,
        mesh=mesh,
        in_specs=placed,
        out_specs=(P("ctx", "exp"), P("ctx", "exp"), P("ctx", "exp")),
        check_vma=False,
    )
```

profile of v0, /device:TPU:2, one launch (start us, length us, event | category | flops | bytes accessed | tf_op | source)
XLA Modules:
  0.0 386.1 jit_solution(18143667295432726540)
XLA Ops:
  8.9 1.4 reduce_window_sum.43
  14.7 1.8 concatenate.6
  16.5 1.9 mul.202
  18.4 2.3 mul.203
  23.2 2.2 convolution_convert_fusion
  25.4 2.9 reshape.141
  28.3 20.9 %all_to_all.10 = bf16[32,2,6144]{2,1,0:T(2,128)(2,1)} all-to-all(bf16[32,2,6144]{2,1,0:T(2,128)(2,1)} %reshape.141), channel_id=1, replica_groups=mesh['ctx'=8,'exp'=32] {'exp'}, dimensions={0} | all-to-all | bytes 1572864 | tf_op jit(solution)/shard_map/all_to_all | solution.py:162
  49.2 3.0 reshape.142
  52.4 74.6 %all-gather.5.cloned.1.call-done = bf16[512,6144]{1,0:T(8,128)(2,1)} async-done(((bf16[64,6144]{1,0:T(8,128)(2,1)}), bf16[512,6144]{1,0:T(8,128)(2,1)}) %all-gather.5.cloned.1.call-update) | async-done | bytes 6291472 | tf_op jit(solution)/shard_map/all_gather | solution.py:166
  127.0 6.1 %fusion.2 = f32[512,576]{0,1:T(8,128)} fusion(bf16[1,3072,576]{1,2,0:T(8,128)(2,1)} %param.27, bf16[512,6144]{1,0:T(8,128)(2,1)} %all-gather.5.cloned.1.call-done), kind=kOutput, calls=%fused_computation.6 | convolution fusion | flops 1811939328 | bytes 7864320 | tf_op jit(solution)/shard_map/dot_general | solution.py:43
  133.1 3.1 fusion.7
  136.2 11.1 %fusion = f32[512,3072]{1,0:T(8,128)} fusion(bf16[1,3072,576]{1,2,0:T(8,128)(2,1)} %param.27, f32[512,576]{0,1:T(8,128)} %fusion.7, bf16[1,3072,576]{1,2,0:T(8,128)(2,1)S(1)} %copy-done, bf16[512,6144]{1,0:T(8,128)(2,1)} %all-gather.5.cloned.1.call-done, f32[512,576]{0,1:T(8,128)} %fusion.2), kind=kOutput, calls=%fused_computation.4 | convolution fusion | flops 3626827776 | bytes 18874368 | tf_op jit(solution)/shard_map/dot_general | solution.py:53
  147.3 6.8 %add_convert_fusion = bf16[512,3072]{1,0:T(8,128)(2,1)} fusion(f32[512,3072]{1,0:T(8,128)} %fusion, bf16[1,3072,576]{1,2,0:T(8,128)(2,1)S(1)} %copy-done, f32[512,576]{0,1:T(8,128)} %fusion.7, f32[512,576]{0,1:T(8,128)} %fusion.2), kind=kOutput, calls=%fused_computation.3 | convolution fusion | flops 1816854528 | bytes 15335424 | tf_op jit(solution)/shard_map/dot_general | solution.py:56
  154.1 7.2 %convert_element_type.79 = bf16[8,32,2,3072]{3,2,1,0:T(2,128)(2,1)} reshape(bf16[512,3072]{1,0:T(8,128)(2,1)} %add_convert_fusion) | data formatting | bytes 6291456 | tf_op jit(solution)/shard_map/convert_element_type | solution.py:170
  161.3 4.4 %copy.34 = bf16[8,32,2,3072]{3,1,2,0:T(8,128)(2,1)} copy(bf16[8,32,2,3072]{3,2,1,0:T(2,128)(2,1)} %convert_element_type.79) | data formatting | bytes 6291456 | tf_op jit(solution)/shard_map/convert_element_type | solution.py:170
  165.7 45.8 %reduce-scatter.2.cloned.1.call-done = bf16[1,32,2,3072]{3,1,2,0:T(8,128)(2,1)} async-done(((bf16[8,32,2,3072]{3,1,2,0:T(8,128)(2,1)}), bf16[1,32,2,3072]{3,1,2,0:T(8,128)(2,1)}) %reduce-scatter.2.cloned.1.call-update) | async-done | bytes 393232 | tf_op jit(solution)/shard_map/reduce_scatter | solution.py:169
  211.6 2.1 copy.35
  213.7 7.3 %all-to-all-start.1 = ((bf16[32,2,3072]{2,1,0:T(2,128)(2,1)}), bf16[32,2,3072]{2,1,0:T(2,128)(2,1)}, u32[]{:S(2)}, u32[]{:S(2)}) async-start(bf16[32,2,3072]{2,1,0:T(2,128)(2,1)} %copy.35), calls=%async_computation.2 | async-start | bytes 786432 | tf_op jit(solution)/shard_map/all_to_all | solution.py:172
  221.0 1.3 iota_compare_fusion.4
  222.4 1.3 eq.47
  223.7 6.3 %all-to-all-done.1 = bf16[32,2,3072]{2,1,0:T(2,128)(2,1)} async-done(((bf16[32,2,3072]{2,1,0:T(2,128)(2,1)}), bf16[32,2,3072]{2,1,0:T(2,128)(2,1)}, u32[]{:S(2)}, u32[]{:S(2)}) %all-to-all-start.1) | async-done | bytes 393248 | tf_op jit(solution)/shard_map/all_to_all | solution.py:172
  230.0 1.9 reshape.153
  231.9 1.2 convolution_reduce_fusion
  234.3 1.8 fusion.64
  238.6 1.3 dynamic-slice
  240.6 16.3 %all-reduce = f32[8]{0:T(128)} all-reduce(f32[8]{0:T(128)S(1)} %dynamic-update-slice), channel_id=1, replica_groups=mesh['ctx'=8,'exp'=32] {'ctx'}, use_global_device_ids=true, to_apply=%add | all-reduce | flops 8 | bytes 64
  257.5 1.6 fusion.53
  259.1 27.3 %all-gather = f32[1024,128]{1,0:T(8,128)} all-gather(f32[128,128]{1,0:T(8,128)S(1)} %fusion.53), channel_id=2, replica_groups=mesh['ctx'=8,'exp'=32] {'ctx'}, dimensions={0}, use_global_device_ids=true | all-gather | bytes 589824 | tf_op jit(solution)/shard_map/all_gather | solution.py:12
  287.0 4.0 %convolution_convert_fusion.1 = bf16[768,128]{1,0:T(8,128)(2,1)S(1)} fusion(bf16[768,3072]{1,0:T(8,128)(2,1)} %all-gather.7.cloned.1.call-done, bf16[128,3072]{1,0:T(8,128)(2,1)} %param.26), kind=kOutput, calls=%fused_computation.42 | convolution fusion | flops 604078080 | bytes 5701632 | tf_op jit(solution)/shard_map/dot_general | solution.py:188
  291.7 1.5 multiply_convert_fusion.1
  293.2 3.2 fusion.22
  296.4 1.6 convolution_multiply_fusion.3
  298.1 49.7 %all-gather.1 = f32[1024,128]{1,0:T(8,128)} all-gather(f32[128,128]{1,0:T(8,128)S(1)} %convolution_multiply_fusion.3), channel_id=3, replica_groups=mesh['ctx'=8,'exp'=32] {'ctx'}, dimensions={0}, use_global_device_ids=true | all-gather | bytes 589824 | tf_op jit(solution)/shard_map/all_gather | solution.py:12
  348.4 23.6 %while.27 = (s32[]{:T(128)}, f32[128,128]{1,0:T(8,128)}, s32[]{:T(128)}, f32[8]{0:T(128)}, f32[8,128,128]{2,1,0:T(8,128)}, /*index=5*/s32[]{:T(128)}, s32[]{:T(128)}, s32[]{:T(128)}, s32[]{:T(128)}) while((s32[]{:T(128)}, f32[128,128]{1,0:T(8,128)}, s32[]{:T(128)}, f32[8]{0:T(128)}, f32[8,128,128]{2,1,0:T(8,128)}, /*index=5*/s32[]{:T(128)}, ...), condition=%wide.region_11.12_spmd, body=%wide.region_10.11_spmd.sunk | while | flops 32774 | bytes 196767 | solution.py:21
  348.4 1.2 dynamic_slice.35
  349.6 2.2 bitcast_add_fusion.5
  351.8 1.2 dynamic_slice.35
  353.0 2.2 bitcast_add_fusion.5
  356.4 2.2 bitcast_add_fusion.5
  358.5 1.2 dynamic_slice.35
  359.8 2.2 bitcast_add_fusion.5
  363.1 2.2 bitcast_add_fusion.5
  366.5 2.2 bitcast_add_fusion.5
  368.7 1.2 dynamic_slice.35
  369.9 2.2 bitcast_add_fusion.5
  372.0 1.4 fusion.34
  373.5 2.1 fusion.42
  375.6 2.5 fusion.41
  (59 shorter events, 20.3 us)
Async XLA Ops:
  7.2 129.1 %copy-start = (bf16[1,3072,576]{1,2,0:T(8,128)(2,1)S(1)}, bf16[1,3072,576]{1,2,0:T(8,128)(2,1)}, u32[]{:S(2)}) copy-start(bf16[1,3072,576]{1,2,0:T(8,128)(2,1)} %param.28) | copy-start | bytes 10616836
  7.2 119.8 %all-gather.5.cloned.1.call-start = ((), (), s32[]{:S(2)}) async-start(), calls=%async_computation.3 | async-start | bytes 7077888 | tf_op jit(solution)/shard_map/all_gather | solution.py:166
  52.2 159.4 %reduce-scatter.2.cloned.1.call-start = ((), (), s32[]{:S(2)}) async-start(), calls=%async_computation.4 | async-start | bytes 3538944 | tf_op jit(solution)/shard_map/reduce_scatter | solution.py:169
  127.0 6.1 %copy-start.8 = (bf16[512,6144]{1,0:T(8,128)(2,1)S(1)}, bf16[512,6144]{1,0:T(8,128)(2,1)}, u32[]{:S(2)}) copy-start(bf16[512,6144]{1,0:T(8,128)(2,1)} %all-gather.5.cloned.1.call-done) | copy-start | bytes 18874372
  127.0 6.1 %copy-start.9 = (bf16[1,576,3072]{2,1,0:T(8,128)(2,1)S(1)}, bf16[1,576,3072]{2,1,0:T(8,128)(2,1)}, u32[]{:S(2)}) copy-start(bf16[1,576,3072]{2,1,0:T(8,128)(2,1)} %param.29) | copy-start | bytes 10616836
  165.7 67.5 %copy-start.7 = (f32[3072]{0:T(1024)S(1)}, f32[3072]{0:T(1024)}, u32[]{:S(2)}) copy-start(f32[3072]{0:T(1024)} %param.22) | copy-start | bytes 36868
  213.7 16.3 %all-to-all-start.1 = ((bf16[32,2,3072]{2,1,0:T(2,128)(2,1)}), bf16[32,2,3072]{2,1,0:T(2,128)(2,1)}, u32[]{:S(2)}, u32[]{:S(2)}) async-start(bf16[32,2,3072]{2,1,0:T(2,128)(2,1)} %copy.35), calls=%async_computation.2 | async-start | bytes 786432 | tf_op jit(solution)/shard_map/all_to_all | solution.py:172
  221.0 66.0 %all-gather.7.cloned.1.call-start = ((), (), s32[]{:S(2)}) async-start(), calls=%async_computation.5 | async-start | bytes 4866048 | tf_op jit(solution)/shard_map/all_gather | solution.py:189
  287.0 4.7 %copy-start.4 = (bf16[768,128]{1,0:T(8,128)(2,1)S(1)}, bf16[768,128]{1,0:T(8,128)(2,1)}, u32[]{:S(2)}) copy-start(bf16[768,128]{1,0:T(8,128)(2,1)} %param.19) | copy-start | bytes 589828
  291.0 0.7 copy-start.5
  372.0 6.0 %copy-start.2 = (f32[128,128]{1,0:T(8,128)S(1)}, f32[128,128]{1,0:T(8,128)}, u32[]{:S(2)}) copy-start(f32[128,128]{1,0:T(8,128)} %get-tuple-element.131) | copy-start | bytes 196612
  372.0 6.0 %copy-start.6 = (bf16[768,128]{1,0:T(8,128)(2,1)S(1)}, bf16[768,128]{1,0:T(8,128)(2,1)}, u32[]{:S(2)}) copy-start(bf16[768,128]{1,0:T(8,128)(2,1)} %copy-done.5) | copy-start | bytes 589828
  372.0 6.4 %copy-start.1 = (bf16[768,768]{1,0:T(8,128)(2,1)S(1)}, bf16[768,768]{1,0:T(8,128)(2,1)}, u32[]{:S(2)}) copy-start(bf16[768,768]{1,0:T(8,128)(2,1)} %multiply_convert_fusion.1) | copy-start | bytes 3538948
  372.0 6.4 %copy-start.3 = (bf16[768,128]{1,0:T(8,128)(2,1)S(1)}, bf16[768,128]{1,0:T(8,128)(2,1)}, u32[]{:S(2)}) copy-start(bf16[768,128]{1,0:T(8,128)(2,1)} %param.18) | copy-start | bytes 589828
Sparse Core Ops, SparseCore 0:
  52.3 74.6 all-gather.4
  165.9 45.6 reduce-scatter.1
  236.2 48.4 all-gather.6
where the time goes:
time: 388 us; the launch traced here: 386 us
  waiting for transfers between devices  127 us (33%)
  blocking collectives  114 us (29%)
  matrix products  50 us (13%)
  local copies, waits for them, and re-layouts  45.2 us (12%)
  other arithmetic  27.8 us (7%)
  between operations  14.5 us (4%)
  starting transfers between devices  7.6 us (2%)
    all_gather x2, blocking collectives, prefix(): gathered = jax.tree.map(lambda a: lax.all_gather(a, axis), part)  77 us
    all_gather x1, waiting for transfers between devices, body(): lax.all_gather(arrived, 'ctx', axis=0, tiled=True)  74.6 us
    reduce_scatter x1, waiting for transfers between devices, body(): lax.psum_scatter(partials.astype(jnp.bfloat16), 'ctx', scatter_dimension=...  45.8 us
    all_to_all x1, blocking collectives, body(): lax.all_to_all(outgoing, 'exp', split_axis=0, concat_axis=0, tiled=True)  20.9 us
    unnamed x1, blocking collectives  16.3 us
    add x7, other arithmetic, chain_link(): return (earlier[0] * following[0], following[0] * earlier[1] + following[1])  15.1 us
    convert_element_type x2, local copies, waits for them, and re-layouts, body(): partials.astype(jnp.bfloat16)  11.6 us
    dot_general x1, matrix products, expert_rows(): lax.dot_general(gate_grad, gate_mat, (((1,), (1,)), ((), ())), preferred_...  11.1 us
  transfers between devices with their start and end apart: 4, of which 3 were waited for; matrix products, arithmetic and copies ran while one was open for 2% of the time, Pallas kernels for 0%

commit v1 on v0

--- a/solution.py
+++ b/solution.py
@@ -162,9 +162,17 @@
     arrived = lax.all_to_all(outgoing, "exp", split_axis=0, concat_axis=0, tiled=True).reshape(
         exp_count * capacity, 2 * features
     )
-    partials = expert_rows(
-        lax.all_gather(arrived, "ctx", axis=0, tiled=True), gate_mat, up_mat, down_mat
-    )
+
+    def obtain_works(values):
+        device_axis = "ctx"
+        n_chips = lax.axis_size(device_axis)
+        pile = tuple((n_chips if i == 0 else 1 for i in range(values.ndim)))
+        state_now = jnp.tile(values, pile)
+        return lax.all_to_all(
+            state_now, axis_name=device_axis, split_axis=0, concat_axis=0, tiled=True
+        )
+
+    partials = expert_rows(obtain_works(arrived), gate_mat, up_mat, down_mat)
     partials = partials.reshape(ctx_count, exp_count, capacity, features)
     summed = lax.psum_scatter(
         partials.astype(jnp.bfloat16), "ctx", scatter_dimension=0, tiled=True

time: 388 us -> 459 us (1.18)
  blocking collectives: 114 us -> 264 us
  waiting for transfers between devices: 127 us -> 47.2 us
    all_to_all x0 -> x1, blocking collectives: none -> 150 us  [obtain_works(): lax.all_to_all(state_now, axis_name=device_axis, split_axis=0, concat_axi...]
    all_gather x1 -> x0, waiting for transfers between devices: 74.6 us -> none  [body(): lax.all_gather(arrived, 'ctx', axis=0, tiled=True)]
    reduce_scatter x1, waiting for transfers between devices: 45.8 us -> 40.9 us  [body(): lax.psum_scatter(partials.astype(jnp.bfloat16), 'ctx', scatter_dimension=...]
    another operation x1 -> x3, local copies, waits for them, and re-layouts: 0.12 us -> 4.97 us  [the longest x2 4.85 us: obtain_works(): state_now = jnp.tile(values, pile)]
  transfers between devices with their start and end apart: 4 -> 3, of which waited for: 3 -> 2; matrix products, arithmetic and copies ran while one was open for 2% -> 2% of each run, Pallas kernels for 0% -> 0%
where the time goes in v1:
time: 459 us; the launch traced here: 457 us
  blocking collectives  264 us (58%)
  local copies, waits for them, and re-layouts  48.7 us (11%)
  waiting for transfers between devices  47.2 us (10%)
  matrix products  47 us (10%)
  other arithmetic  27.7 us (6%)
  between operations  14.8 us (3%)
  starting transfers between devices  7.51 us (2%)
    all_to_all x1, blocking collectives, obtain_works(): lax.all_to_all(state_now, axis_name=device_axis, split_axis=0, concat_axi...  150 us
    all_gather x2, blocking collectives, prefix(): gathered = jax.tree.map(lambda a: lax.all_gather(a, axis), part)  77.1 us
    reduce_scatter x1, waiting for transfers between devices, body(): lax.psum_scatter(partials.astype(jnp.bfloat16), 'ctx', scatter_dimension=...  40.9 us
    all_to_all x1, blocking collectives, body(): lax.all_to_all(outgoing, 'exp', split_axis=0, concat_axis=0, tiled=True)  20.9 us
    unnamed x1, blocking collectives  16.1 us
    add x7, other arithmetic, chain_link(): return (earlier[0] * following[0], following[0] * earlier[1] + following[1])  15.1 us
    convert_element_type x2, local copies, waits for them, and re-layouts, body(): partials.astype(jnp.bfloat16)  11.7 us
    dot_general x1, matrix products, expert_rows(): lax.dot_general(gate_grad, gate_mat, (((1,), (1,)), ((), ())), preferred_...  11.1 us
  transfers between devices with their start and end apart: 3, of which 2 were waited for; matrix products, arithmetic and copies ran while one was open for 2% of the time, Pallas kernels for 0%

profile of v1, /device:TPU:2, one launch (start us, length us, event | category | flops | bytes accessed | tf_op | source)
XLA Modules:
  0.0 457.3 jit_solution(12713695408041742184)
XLA Ops:
  8.9 1.4 reduce_window_sum.43
  14.7 1.8 concatenate.6
  16.5 1.9 mul.202
  18.4 2.3 mul.203
  23.2 2.2 convolution_convert_fusion
  25.4 2.9 reshape.145
  28.3 20.9 %all_to_all.19 = bf16[32,2,6144]{2,1,0:T(2,128)(2,1)} all-to-all(bf16[32,2,6144]{2,1,0:T(2,128)(2,1)} %reshape.145), channel_id=1, replica_groups=mesh['ctx'=8,'exp'=32] {'exp'}, dimensions={0} | all-to-all | bytes 1572864 | tf_op jit(solution)/shard_map/all_to_all | solution.py:162
  49.2 3.0 tile.8
  52.1 1.9 tile.9
  54.0 150.1 %all_to_all.20 = bf16[8,64,6144]{2,1,0:T(8,128)(2,1)S(1)} all-to-all(bf16[8,64,6144]{2,1,0:T(8,128)(2,1)S(1)} %tile.9), channel_id=1, replica_groups=mesh['ctx'=8,'exp'=32] {'ctx'}, dimensions={0} | all-to-all | bytes 12582912 | tf_op jit(solution)/shard_map/all_to_all | solution.py:171
  204.2 3.0 fusion.2
  208.8 3.1 fusion.7
  211.9 11.1 %fusion = f32[512,3072]{1,0:T(8,128)} fusion(bf16[1,3072,576]{1,2,0:T(8,128)(2,1)} %param.27, f32[512,576]{0,1:T(8,128)} %fusion.7, bf16[1,3072,576]{1,2,0:T(8,128)(2,1)S(1)} %copy-done, bf16[512,6144]{1,0:T(8,128)(2,1)} %bitcast.78, f32[512,576]{0,1:T(8,128)} %fusion.2), kind=kOutput, calls=%fused_computation.4 | convolution fusion | flops 3626827776 | bytes 18874368 | tf_op jit(solution)/shard_map/dot_general | solution.py:53
  223.0 6.9 %add_convert_fusion = bf16[512,3072]{1,0:T(8,128)(2,1)} fusion(f32[512,3072]{1,0:T(8,128)} %fusion, bf16[1,3072,576]{1,2,0:T(8,128)(2,1)S(1)} %copy-done, f32[512,576]{0,1:T(8,128)} %fusion.7, f32[512,576]{0,1:T(8,128)} %fusion.2), kind=kOutput, calls=%fused_computation.3 | convolution fusion | flops 1816854528 | bytes 15335424 | tf_op jit(solution)/shard_map/dot_general | solution.py:56
  229.8 7.2 %convert_element_type.79 = bf16[8,32,2,3072]{3,2,1,0:T(2,128)(2,1)} reshape(bf16[512,3072]{1,0:T(8,128)(2,1)} %add_convert_fusion) | data formatting | bytes 6291456 | tf_op jit(solution)/shard_map/convert_element_type | solution.py:178
  237.1 4.4 copy.34
  241.5 40.9 %reduce-scatter.2.cloned.1.call-done = bf16[1,32,2,3072]{3,1,2,0:T(8,128)(2,1)} async-done(((bf16[8,32,2,3072]{3,1,2,0:T(8,128)(2,1)}), bf16[1,32,2,3072]{3,1,2,0:T(8,128)(2,1)}) %reduce-scatter.2.cloned.1.call-update) | async-done | bytes 393232 | tf_op jit(solution)/shard_map/reduce_scatter | solution.py:177
  282.4 2.1 copy.35
  284.5 7.4 %all-to-all-start.2 = ((bf16[32,2,3072]{2,1,0:T(2,128)(2,1)}), bf16[32,2,3072]{2,1,0:T(2,128)(2,1)}, u32[]{:S(2)}, u32[]{:S(2)}) async-start(bf16[32,2,3072]{2,1,0:T(2,128)(2,1)} %copy.35), calls=%async_computation.3 | async-start | bytes 786432 | tf_op jit(solution)/shard_map/all_to_all | solution.py:180
  292.0 1.3 iota_compare_fusion.4
  293.3 1.3 eq.47
  294.6 6.3 %all-to-all-done.2 = bf16[32,2,3072]{2,1,0:T(2,128)(2,1)} async-done(((bf16[32,2,3072]{2,1,0:T(2,128)(2,1)}), bf16[32,2,3072]{2,1,0:T(2,128)(2,1)}, u32[]{:S(2)}, u32[]{:S(2)}) %all-to-all-start.2) | async-done | bytes 393248 | tf_op jit(solution)/shard_map/all_to_all | solution.py:180
  301.0 1.9 reshape.156
  302.9 1.2 convolution_reduce_fusion
  305.3 1.8 fusion.64
  309.5 1.3 dynamic-slice
  311.6 16.1 %all-reduce = f32[8]{0:T(128)} all-reduce(f32[8]{0:T(128)S(1)} %dynamic-update-slice), channel_id=1, replica_groups=mesh['ctx'=8,'exp'=32] {'ctx'}, use_global_device_ids=true, to_apply=%add | all-reduce | flops 8 | bytes 64
  328.2 1.6 fusion.53
  329.9 27.3 %all-gather = f32[1024,128]{1,0:T(8,128)} all-gather(f32[128,128]{1,0:T(8,128)S(1)} %fusion.53), channel_id=2, replica_groups=mesh['ctx'=8,'exp'=32] {'ctx'}, dimensions={0}, use_global_device_ids=true | all-gather | bytes 589824 | tf_op jit(solution)/shard_map/all_gather | solution.py:12
  357.8 4.0 convolution_convert_fusion.1
  362.5 1.5 multiply_convert_fusion.1
  364.0 3.2 fusion.22
  367.2 1.6 convolution_multiply_fusion.3
  368.9 49.8 %all-gather.1 = f32[1024,128]{1,0:T(8,128)} all-gather(f32[128,128]{1,0:T(8,128)S(1)} %convolution_multiply_fusion.3), channel_id=3, replica_groups=mesh['ctx'=8,'exp'=32] {'ctx'}, dimensions={0}, use_global_device_ids=true | all-gather | bytes 589824 | tf_op jit(solution)/shard_map/all_gather | solution.py:12
  419.3 23.6 %while.27 = (s32[]{:T(128)}, f32[128,128]{1,0:T(8,128)}, s32[]{:T(128)}, f32[8]{0:T(128)}, f32[8,128,128]{2,1,0:T(8,128)}, /*index=5*/s32[]{:T(128)}, s32[]{:T(128)}, s32[]{:T(128)}, s32[]{:T(128)}) while((s32[]{:T(128)}, f32[128,128]{1,0:T(8,128)}, s32[]{:T(128)}, f32[8]{0:T(128)}, f32[8,128,128]{2,1,0:T(8,128)}, /*index=5*/s32[]{:T(128)}, ...), condition=%wide.region_11.12_spmd, body=%wide.region_10.11_spmd.sunk | while | flops 32774 | bytes 196767 | solution.py:21
  419.3 1.2 dynamic_slice.35
  420.5 2.2 bitcast_add_fusion.5
  422.6 1.2 dynamic_slice.35
  423.9 2.2 bitcast_add_fusion.5
  427.2 2.2 bitcast_add_fusion.5
  430.6 2.2 bitcast_add_fusion.5
  432.8 1.2 dynamic_slice.35
  434.0 2.2 bitcast_add_fusion.5
  437.3 2.2 bitcast_add_fusion.5
  440.7 2.2 bitcast_add_fusion.5
  442.9 1.4 fusion.34
  444.3 2.1 fusion.42
  446.4 2.5 fusion.41
  (60 shorter events, 22.9 us)
Async XLA Ops:
  7.2 204.7 %copy-start = (bf16[1,3072,576]{1,2,0:T(8,128)(2,1)S(1)}, bf16[1,3072,576]{1,2,0:T(8,128)(2,1)}, u32[]{:S(2)}) copy-start(bf16[1,3072,576]{1,2,0:T(8,128)(2,1)} %param.28) | copy-start | bytes 10616836
  7.2 275.2 %reduce-scatter.2.cloned.1.call-start = ((), (), s32[]{:S(2)}) async-start(), calls=%async_computation.4 | async-start | bytes 3538944 | tf_op jit(solution)/shard_map/reduce_scatter | solution.py:177
  54.0 150.2 %copy-start.10 = (bf16[1,3072,576]{1,2,0:T(8,128)(2,1)S(1)}, bf16[1,3072,576]{1,2,0:T(8,128)(2,1)}, u32[]{:S(2)}) copy-start(bf16[1,3072,576]{1,2,0:T(8,128)(2,1)} %param.27) | copy-start | bytes 10616836
  204.2 3.7 copy-start.1
  204.2 4.6 %copy-start.9 = (bf16[1,576,3072]{2,1,0:T(8,128)(2,1)S(1)}, bf16[1,576,3072]{2,1,0:T(8,128)(2,1)}, u32[]{:S(2)}) copy-start(bf16[1,576,3072]{2,1,0:T(8,128)(2,1)} %param.29) | copy-start | bytes 10616836
  241.5 62.7 %copy-start.8 = (f32[3072]{0:T(1024)S(1)}, f32[3072]{0:T(1024)}, u32[]{:S(2)}) copy-start(f32[3072]{0:T(1024)} %param.22) | copy-start | bytes 36868
  284.5 16.5 %all-to-all-start.2 = ((bf16[32,2,3072]{2,1,0:T(2,128)(2,1)}), bf16[32,2,3072]{2,1,0:T(2,128)(2,1)}, u32[]{:S(2)}, u32[]{:S(2)}) async-start(bf16[32,2,3072]{2,1,0:T(2,128)(2,1)} %copy.35), calls=%async_computation.3 | async-start | bytes 786432 | tf_op jit(solution)/shard_map/all_to_all | solution.py:180
  292.0 65.9 %all-gather.4.cloned.1.call-start = ((), (), s32[]{:S(2)}) async-start(), calls=%async_computation.5 | async-start | bytes 4866048 | tf_op jit(solution)/shard_map/all_gather | solution.py:197
  357.8 4.7 %copy-start.5 = (bf16[768,128]{1,0:T(8,128)(2,1)S(1)}, bf16[768,128]{1,0:T(8,128)(2,1)}, u32[]{:S(2)}) copy-start(bf16[768,128]{1,0:T(8,128)(2,1)} %param.19) | copy-start | bytes 589828
  361.8 0.7 copy-start.6
  442.9 6.0 %copy-start.3 = (f32[128,128]{1,0:T(8,128)S(1)}, f32[128,128]{1,0:T(8,128)}, u32[]{:S(2)}) copy-start(f32[128,128]{1,0:T(8,128)} %get-tuple-element.131) | copy-start | bytes 196612
  442.9 6.0 %copy-start.7 = (bf16[768,128]{1,0:T(8,128)(2,1)S(1)}, bf16[768,128]{1,0:T(8,128)(2,1)}, u32[]{:S(2)}) copy-start(bf16[768,128]{1,0:T(8,128)(2,1)} %copy-done.6) | copy-start | bytes 589828
  442.9 6.4 %copy-start.2 = (bf16[768,768]{1,0:T(8,128)(2,1)S(1)}, bf16[768,768]{1,0:T(8,128)(2,1)}, u32[]{:S(2)}) copy-start(bf16[768,768]{1,0:T(8,128)(2,1)} %multiply_convert_fusion.1) | copy-start | bytes 3538948
  442.9 6.4 %copy-start.4 = (bf16[768,128]{1,0:T(8,128)(2,1)S(1)}, bf16[768,128]{1,0:T(8,128)(2,1)}, u32[]{:S(2)}) copy-start(bf16[768,128]{1,0:T(8,128)(2,1)} %param.18) | copy-start | bytes 589828
Sparse Core Ops, SparseCore 0:
  241.6 40.6 reduce-scatter.1
  307.2 48.2 all-gather.3
